TPU v7x, 32 devices: a whole 2x2x4 slice. The times are simulated.
32 devices in a mesh: prow: 8 (over y, x, core), pcol: 4 (over z).
Axes of the slice: x: 2, y: 2, z: 4, core: 2. Of those that a mesh axis runs over, the one named last changes fastest.
Arguments:
- matrix: float32 [4096, 4096], P('prow', 'pcol'), may hold values from -6 to 6
- pivots: int32 [2, 512], replicated, may hold values from 0 to 4095, as said below
- lower_inv: float32 [2, 512, 512], replicated, as said below
- upper_inv: float32 [2, 512, 512], replicated, as said below
Outputs:
- factored: float32 [4096, 4096], P('prow', 'pcol')
Inputs may be any that keep to these rules, and one draw needn't show every extreme that they name: The entries of pivots[k] are distinct row indices from k * 512 to 4095. Each lower_inv[k] is lower triangular. Each upper_inv[k] is upper triangular.
All inputs are finite; a program needn't handle non-finite values.
Results may differ from a plain program's by a relative error of at most 0.0001.
Values sent between devices are 32-bit elements; how exact they have to be, the bound alone decides.
No kernel may reach another device: no remote copies, remote signals or barrier semaphores. Data moves between devices by JAX's collectives and lax.ppermute only.
A program may use at most 128 MiB of HBM per device.

v0:
```python
import jax
import jax.numpy as jnp
from jax import lax
from jax.sharding import PartitionSpec as P


def broadcast(block, axis, holder):
    block = jnp.where(lax.axis_index(axis) == holder, block, jnp.zeros_like(block))
    return lax.psum(block, axis)


def displaced(pivot_row, start_row):
    width = pivot_row.shape[0]
    end_row = start_row + width
    window = start_row + jnp.arange(width, dtype=jnp.int32)
    chosen = jnp.any(pivot_row[None, :] == window[:, None], axis=1)
    unnamed = jnp.logical_not(chosen)
    free_rank = jnp.cumsum(unnamed.astype(jnp.int32)) - 1
    outside = pivot_row >= end_row
    out_rank = jnp.sum(
        (outside[None, :] & (pivot_row[None, :] < pivot_row[:, None])).astype(jnp.int32), axis=1
    )
    matches = unnamed[None, :] & (free_rank[None, :] == out_rank[:, None])
    source = jnp.sum(jnp.where(matches, window[None, :], 0), axis=1)
    return (source, outside)


def product(left, right):
    return jnp.dot(left, right, precision=lax.Precision.HIGHEST, preferred_element_type=jnp.float32)


def shards(matrix, pivots, lower_inv, upper_inv):
    local_rows, local_cols = matrix.shape
    block_width = lower_inv.shape[1]
    first_row = lax.axis_index("prow") * local_rows
    row_ids = first_row + jnp.arange(local_rows, dtype=jnp.int32)
    col_ids = lax.axis_index("pcol") * local_cols + jnp.arange(local_cols, dtype=jnp.int32)
    current = matrix
    for panel_index in range(pivots.shape[0]):
        start_row = panel_index * block_width
        end_row = start_row + block_width
        wanted = pivots[panel_index]
        offset = wanted - first_row
        owned_rows = (offset >= 0) & (offset < local_rows)
        gathered_rows = jnp.take(current, jnp.clip(offset, 0, local_rows - 1), axis=0)
        picked = jnp.where(owned_rows[:, None], gathered_rows, 0.0)
        beyond = col_ids >= end_row
        reduced = lax.psum_scatter(picked, "prow", scatter_dimension=0, tiled=True)
        raw_top = lax.all_gather(reduced, "prow", axis=0, tiled=True)
        solved = product(lower_inv[panel_index], raw_top)
        top_block = jnp.where(beyond[None, :], solved, raw_top)
        top_masked = jnp.where(beyond[None, :], solved, 0.0)
        owner_row = start_row // local_rows
        first_local = start_row - owner_row * local_rows
        local_top = current
        old_top = broadcast(local_top, "prow", owner_row)
        source, outside = displaced(wanted, start_row)
        dest_local = jnp.where(outside & owned_rows, offset, local_rows)
        moved = jnp.take(old_top, jnp.clip(source - start_row, 0, block_width - 1), axis=0)
        swapped = current.at[dest_local].set(moved, mode="drop")
        is_owner = lax.axis_index("prow") == owner_row
        top_slice = swapped
        swapped = swapped.at[first_local : first_local + block_width].set(
            jnp.where(is_owner, top_block, top_slice)
        )
        owner_col = start_row // local_cols
        left_col = start_row - owner_col * local_cols
        column_panel = product(
            swapped[:, left_col : left_col + block_width], upper_inv[panel_index]
        )
        lower_block = broadcast(column_panel, "pcol", owner_col)
        below_rows = row_ids >= end_row
        lower_masked = jnp.where(below_rows[:, None], lower_block, 0.0)
        updated = swapped - product(lower_masked, top_masked)
        panel_slice = updated[:, left_col : left_col + block_width]
        col_owner = lax.axis_index("pcol") == owner_col
        new_panel = jnp.where(below_rows[:, None] & col_owner, lower_block, panel_slice)
        current = updated.at[:, left_col : left_col + block_width].set(new_panel)
    return current


def solution(mesh):
    in_specs = (P("prow", "pcol"), P(), P(), P())
    out_specs = P("prow", "pcol")
    return jax.shard_map(shards, mesh=mesh, in_specs=in_specs, out_specs=out_specs, check_vma=False)
```

profile of v0, /device:TPU:0, one launch (start us, length us, event | category | flops | bytes accessed | tf_op | source)
XLA Modules:
  0.0 474.5 jit_solution(15905027569336554562)
XLA Ops:
  10.8 2.9 copy.50
  13.8 3.2 select_select_fusion.1
  17.0 2.9 copy.72
  21.8 3.1 broadcast_select_fusion.1
  25.0 39.0 %reduce-scatter.7.cloned.1.call-done = f32[64,1024]{1,0:T(8,128)} async-done(((f32[512,1024]{1,0:T(8,128)}), f32[64,1024]{1,0:T(8,128)}) %reduce-scatter.7.cloned.1.call-update) | async-done | bytes 262160 | tf_op jit(solution)/shard_map/reduce_scatter | solution.py:48
  65.9 63.2 %all-reduce.5.cloned.1.call-done = f32[512,1024]{0,1:T(8,128)} async-done(((f32[512,1024]{0,1:T(8,128)}), f32[512,1024]{0,1:T(8,128)}) %all-reduce.5.cloned.1.call-update) | async-done | bytes 2097168 | tf_op jit(solution)/shard_map/psum | solution.py:9
  131.9 19.5 %scatter_custom_fusion = f32[512,1024]{1,0:T(8,128)S(1)} fusion(f32[512,1024]{1,0:T(8,128)S(1)} %copy.85, s32[512]{0:T(512)S(1)} %bitcast.75, f32[]{:T(128)} %constant.160.clone.4, pred[512]{0:T(512)(128)(4,1)S(1)} %compare_and_fusion.2, f32[512,1024]{1,0:T(8,128)} %copy.54, s32[1024]{0:T(1024)S(1)} %pad_clamp_fusion.2), kind=kCustom, calls=%fused_computation.17 | custom fusion | flops 524288 | bytes 4198916 | tf_op jit(solution)/shard_map/scatter | solution.py:60
  153.2 5.0 %all-gather.3.cloned.1.call-done = f32[512,1024]{1,0:T(8,128)} async-done(((f32[64,1024]{1,0:T(8,128)}), f32[512,1024]{1,0:T(8,128)}) %all-gather.3.cloned.1.call-update) | async-done | bytes 2097168 | tf_op jit(solution)/shard_map/all_gather | solution.py:49
  158.2 2.9 copy.52
  161.1 10.8 %fusion.2 = (f32[512,1024]{0,1:T(8,128)S(1)}, f32[1024,512]{1,0:T(8,128)}) fusion(f32[512,1024]{0,1:T(8,128)} %copy.55, f32[512,1024]{0,1:T(8,128)} %copy.52, pred[1024]{0:T(1024)(128)(4,1)S(1)} %fusion.41, pred[]{:T(512)S(6)} %eq.31, f32[512,1024]{1,0:T(8,128)} %all-gather.3.cloned.1.call-done, f32[2,512,512]{2,1,0:T(8,128)} %param.20), kind=kOutput, calls=%fused_computation.12 | convolution fusion | flops 3222274048 | bytes 11535361 | tf_op jit(solution)/shard_map/dot_general | solution.py:29
  171.9 2.9 convolution_select_fusion.1
  175.7 51.7 %all-reduce.7.cloned.1.call-done = f32[512,512]{0,1:T(8,128)} async-done(((f32[512,512]{0,1:T(8,128)}), f32[512,512]{0,1:T(8,128)}) %all-reduce.7.cloned.1.call-update) | async-done | bytes 1048592 | tf_op jit(solution)/shard_map/psum | solution.py:9
  227.4 6.9 %fusion.8 = f32[512,1024]{0,1:T(8,128)} fusion(f32[512,1024]{0,1:T(8,128)S(1)} %get-tuple-element.86, f32[1024,512]{1,0:T(8,128)} %get-tuple-element.87, f32[512,512]{0,1:T(8,128)} %all-reduce.7.cloned.1.call-done, pred[1024]{0:T(1024)(128)(4,1)S(1)} %fusion.41, pred[512]{0:T(512)(128)(4,1)S(1)} %fusion.44), kind=kOutput, calls=%fused_computation.20 | convolution fusion | flops 3222536192 | bytes 7341568 | tf_op jit(solution)/shard_map/dot_general | solution.py:29
  234.3 3.0 fusion.10
  244.8 3.2 select_select_fusion
  252.6 39.1 %reduce-scatter.9.cloned.1.call-done = f32[64,1024]{1,0:T(8,128)} async-done(((f32[512,1024]{1,0:T(8,128)}), f32[64,1024]{1,0:T(8,128)}) %reduce-scatter.9.cloned.1.call-update) | async-done | bytes 262160 | tf_op jit(solution)/shard_map/reduce_scatter | solution.py:48
  293.0 63.5 %all-reduce.9.cloned.1.call-done = f32[512,1024]{0,1:T(8,128)} async-done(((f32[512,1024]{0,1:T(8,128)}), f32[512,1024]{0,1:T(8,128)}) %all-reduce.9.cloned.1.call-update) | async-done | bytes 2097168 | tf_op jit(solution)/shard_map/psum | solution.py:9
  359.4 19.6 %scatter_custom_fusion.1 = f32[512,1024]{1,0:T(8,128)S(1)} fusion(f32[512,1024]{1,0:T(8,128)S(1)} %copy.58, s32[512]{0:T(512)S(1)} %bitcast.74, f32[]{:T(128)} %constant.160.clone.4, pred[512]{0:T(512)(128)(4,1)S(1)} %compare_and_fusion, f32[512,1024]{1,0:T(8,128)} %copy.62, s32[1024]{0:T(1024)S(1)} %pad_clamp_fusion), kind=kCustom, calls=%fused_computation.14 | custom fusion | flops 524288 | bytes 4198916 | tf_op jit(solution)/shard_map/scatter | solution.py:60
  380.8 4.9 %all-gather.5.cloned.1.call-done = f32[512,1024]{1,0:T(8,128)} async-done(((f32[64,1024]{1,0:T(8,128)}), f32[512,1024]{1,0:T(8,128)}) %all-gather.5.cloned.1.call-update) | async-done | bytes 2097168 | tf_op jit(solution)/shard_map/all_gather | solution.py:49
  385.7 3.1 copy.61
  388.8 11.4 %fusion = (f32[512,1024]{0,1:T(8,128)S(1)}, f32[1024,512]{1,0:T(8,128)}) fusion(f32[512,1024]{0,1:T(8,128)} %copy.64, f32[512,1024]{0,1:T(8,128)} %copy.61, pred[1024]{0:T(1024)(128)(4,1)S(1)} %fusion.42, pred[]{:T(512)S(6)} %eq.30, f32[512,1024]{1,0:T(8,128)} %all-gather.5.cloned.1.call-done, f32[2,512,512]{2,1,0:T(8,128)} %param.20), kind=kOutput, calls=%fused_computation.8 | convolution fusion | flops 3222274048 | bytes 11535361 | tf_op jit(solution)/shard_map/dot_general | solution.py:29
  400.3 2.9 convolution_select_fusion
  403.2 51.9 %all-reduce.11.cloned.1.call-done = f32[512,512]{0,1:T(8,128)} async-done(((f32[512,512]{0,1:T(8,128)}), f32[512,512]{0,1:T(8,128)}) %all-reduce.11.cloned.1.call-update) | async-done | bytes 1048592 | tf_op jit(solution)/shard_map/psum | solution.py:9
  455.2 6.9 %fusion.9 = f32[512,1024]{0,1:T(8,128)} fusion(f32[512,1024]{0,1:T(8,128)S(1)} %get-tuple-element.88, f32[1024,512]{1,0:T(8,128)} %get-tuple-element.89, f32[512,512]{0,1:T(8,128)} %all-reduce.11.cloned.1.call-done, pred[1024]{0:T(1024)(128)(4,1)S(1)} %fusion.42, pred[512]{0:T(512)(128)(4,1)S(1)} %fusion.43), kind=kOutput, calls=%fused_computation.21 | convolution fusion | flops 3222536192 | bytes 7341568 | tf_op jit(solution)/shard_map/dot_general | solution.py:29
  (78 shorter events, 37.1 us)
Async XLA Ops:
  6.5 1.6 copy-start.4
  6.5 57.4 %reduce-scatter.7.cloned.1.call-start = ((), (), s32[]{:S(2)}) async-start(), calls=%async_computation.8 | async-start | bytes 2359296 | tf_op jit(solution)/shard_map/reduce_scatter | solution.py:48
  19.9 109.1 %all-reduce.5.cloned.1.call-start = ((), (), s32[]{:S(2)}) async-start(), calls=%async_computation.3 | async-start | bytes 4194304 | tf_op jit(solution)/shard_map/psum | solution.py:9
  25.0 133.2 %all-gather.3.cloned.1.call-start = ((), (), s32[]{:S(2)}) async-start(), calls=%async_computation.2 | async-start | bytes 2359296 | tf_op jit(solution)/shard_map/all_gather | solution.py:49
  64.0 163.4 %all-reduce.7.cloned.1.call-start = ((), (), s32[]{:S(2)}) async-start(), calls=%async_computation.4 | async-start | bytes 2097152 | tf_op jit(solution)/shard_map/psum | solution.py:9
  161.1 10.8 %copy-start.2 = (f32[2,512,512]{2,1,0:T(8,128)S(1)}, f32[2,512,512]{2,1,0:T(8,128)}, u32[]{:S(2)}) copy-start(f32[2,512,512]{2,1,0:T(8,128)} %param.21) | copy-start | bytes 6291460
  174.8 116.8 %reduce-scatter.9.cloned.1.call-start = ((), (), s32[]{:S(2)}) async-start(), calls=%async_computation.9 | async-start | bytes 2359296 | tf_op jit(solution)/shard_map/reduce_scatter | solution.py:48
  227.4 6.9 %copy-start = (f32[512,512]{0,1:T(8,128)S(1)}, f32[512,512]{0,1:T(8,128)}, u32[]{:S(2)}) copy-start(f32[512,512]{0,1:T(8,128)} %all-reduce.7.cloned.1.call-done) | copy-start | bytes 3145732
  250.9 105.7 %all-reduce.9.cloned.1.call-start = ((), (), s32[]{:S(2)}) async-start(), calls=%async_computation.6 | async-start | bytes 4194304 | tf_op jit(solution)/shard_map/psum | solution.py:9
  252.5 133.2 %all-gather.5.cloned.1.call-start = ((), (), s32[]{:S(2)}) async-start(), calls=%async_computation.5 | async-start | bytes 2359296 | tf_op jit(solution)/shard_map/all_gather | solution.py:49
  291.7 163.5 %all-reduce.11.cloned.1.call-start = ((), (), s32[]{:S(2)}) async-start(), calls=%async_computation.7 | async-start | bytes 2097152 | tf_op jit(solution)/shard_map/psum | solution.py:9
  388.8 11.4 %copy-start.3 = (f32[2,512,512]{2,1,0:T(8,128)S(1)}, f32[2,512,512]{2,1,0:T(8,128)}, u32[]{:S(2)}) copy-start(f32[2,512,512]{2,1,0:T(8,128)} %param.21) | copy-start | bytes 6291460
  455.2 6.9 %copy-start.1 = (f32[512,512]{0,1:T(8,128)S(1)}, f32[512,512]{0,1:T(8,128)}, u32[]{:S(2)}) copy-start(f32[512,512]{0,1:T(8,128)} %all-reduce.11.cloned.1.call-done) | copy-start | bytes 3145732
Sparse Core Ops, SparseCore 0:
  20.0 43.8 reduce-scatter.6
  67.5 61.4 all-reduce.4
  131.1 27.0 all-gather.2
  175.0 52.4 all-reduce.6
  251.0 40.5 reduce-scatter.8
  295.1 61.4 all-reduce.8
  358.6 27.0 all-gather.4
  403.3 51.8 all-reduce.10
where the time goes:
time: 482 us; the launch traced here: 474 us
  waiting for transfers between devices  318 us (66%)
  other arithmetic  59 us (12%)
  matrix products  41.9 us (9%)
  local copies, waits for them, and re-layouts  41 us (9%)
  between operations  13.9 us (3%)
    psum x4, waiting for transfers between devices, broadcast(): return lax.psum(block, axis)  230 us
    reduce_scatter x2, waiting for transfers between devices, shards(): reduced = lax.psum_scatter(picked, 'prow', scatter_dimension=0, tiled=True)  78 us
    dot_general x6, matrix products, product(): jnp.dot(left, right, precision=lax.Precision.HIGHEST, preferred_element_t...  41.9 us
    scatter x2, other arithmetic, shards(): swapped = current.at[dest_local].set(moved, mode='drop')  39.1 us
    gather x4, local copies, waits for them, and re-layouts, shards(): jnp.take(current, jnp.clip(offset, 0, local_rows - 1), axis=0)  11.1 us
    all_gather x2, waiting for transfers between devices, shards(): raw_top = lax.all_gather(reduced, 'prow', axis=0, tiled=True)  9.83 us
  transfers between devices with their start and end apart: 8, of which 8 were waited for; matrix products, arithmetic and copies ran while one was open for 12% of the time, Pallas kernels for 0%

commit v1 on v0

--- a/solution.py
+++ b/solution.py
@@ -46,7 +46,26 @@
         picked = jnp.where(owned_rows[:, None], gathered_rows, 0.0)
         beyond = col_ids >= end_row
         reduced = lax.psum_scatter(picked, "prow", scatter_dimension=0, tiled=True)
-        raw_top = lax.all_gather(reduced, "prow", axis=0, tiled=True)
+        size, place, width_2 = (lax.axis_size("prow"), lax.axis_index("prow"), reduced.shape[0])
+        right_2 = [(i, (i + 1) % size) for i in range(size)]
+        left_2 = [(i, (i - 1) % size) for i in range(size)]
+        filled = jnp.zeros(
+            (*reduced.shape[:0], size * width_2, *reduced.shape[0 + 1 :]), reduced.dtype
+        )
+        filled = lax.dynamic_update_slice_in_dim(filled, reduced, place * width_2, axis=0)
+        from_left = from_right = reduced
+        middle = size // 2
+        for step in range(1, middle + 1):
+            from_left = lax.ppermute(from_left, "prow", right_2)
+            filled = lax.dynamic_update_slice_in_dim(
+                filled, from_left, (place - step) % size * width_2, axis=0
+            )
+            if step < size - middle:
+                from_right = lax.ppermute(from_right, "prow", left_2)
+                filled = lax.dynamic_update_slice_in_dim(
+                    filled, from_right, (place + step) % size * width_2, axis=0
+                )
+        raw_top = filled
         solved = product(lower_inv[panel_index], raw_top)
         top_block = jnp.where(beyond[None, :], solved, raw_top)
         top_masked = jnp.where(beyond[None, :], solved, 0.0)

time: 482 us -> 543 us (1.13)
  local copies, waits for them, and re-layouts: 41 us -> 99.6 us
  starting transfers between devices: 0.46 us -> 17.3 us
  waiting for transfers between devices: 318 us -> 308 us
  matrix products: 41.9 us -> 35.3 us
    unnamed x8, waiting for transfers between devices: 0.13 us -> 78.3 us
    reduce_scatter x2 -> x0, waiting for transfers between devices: 78 us -> none  [shards(): reduced = lax.psum_scatter(picked, 'prow', scatter_dimension=0, tiled=True)]
    psum x4, waiting for transfers between devices: 230 us -> 152 us  [broadcast(): return lax.psum(block, axis)]
    ppermute x0 -> x14, waiting for transfers between devices: none -> 77.1 us  [the longest x8 50.9 us: shards(): from_left = lax.ppermute(from_left, 'prow', right_2)]
    dynamic_update_slice x0 -> x16, local copies, waits for them, and re-layouts: none -> 59.2 us  [the longest x8 28.4 us: shards(): lax.dynamic_update_slice_in_dim(filled, from_left, (place - step) % size...]
    ppermute x0 -> x14, starting transfers between devices: none -> 16.9 us  [the longest x6 16.8 us: shards(): from_right = lax.ppermute(from_right, 'prow', left_2)]
    all_gather x2 -> x0, waiting for transfers between devices: 9.83 us -> none  [shards(): raw_top = lax.all_gather(reduced, 'prow', axis=0, tiled=True)]
    dot_general x6, matrix products: 41.9 us -> 35.3 us  [product(): jnp.dot(left, right, precision=lax.Precision.HIGHEST, preferred_element_t...]
  transfers between devices with their start and end apart: 8 -> 20, of which waited for: 8 -> 16; matrix products, arithmetic and copies ran while one was open for 12% -> 22% of each run, Pallas kernels for 0% -> 0%
where the time goes in v1:
time: 543 us; the launch traced here: 534 us
  waiting for transfers between devices  308 us (57%)
  local copies, waits for them, and re-layouts  99.6 us (18%)
  other arithmetic  59.2 us (11%)
  matrix products  35.3 us (7%)
  starting transfers between devices  17.3 us (3%)
  between operations  14.3 us (3%)
    psum x4, waiting for transfers between devices, broadcast(): return lax.psum(block, axis)  152 us
    unnamed x8, waiting for transfers between devices  78.3 us
    ppermute x8, waiting for transfers between devices, shards(): from_left = lax.ppermute(from_left, 'prow', right_2)  50.9 us
    scatter x2, other arithmetic, shards(): swapped = current.at[dest_local].set(moved, mode='drop')  39.3 us
    dot_general x6, matrix products, product(): jnp.dot(left, right, precision=lax.Precision.HIGHEST, preferred_element_t...  35.3 us
    dynamic_update_slice x8, local copies, waits for them, and re-layouts, shards(): lax.dynamic_update_slice_in_dim(filled, from_left, (place - step) % size...  28.4 us
    ppermute x6, waiting for transfers between devices, shards(): from_right = lax.ppermute(from_right, 'prow', left_2)  26.2 us
    dynamic_update_slice x6, local copies, waits for them, and re-layouts, shards(): lax.dynamic_update_slice_in_dim(filled, from_right, (place + step) % size...  23.6 us
  transfers between devices with their start and end apart: 20, of which 16 were waited for; matrix products, arithmetic and copies ran while one was open for 22% of the time, Pallas kernels for 0%

profile of v1, /device:TPU:0, one launch (start us, length us, event | category | flops | bytes accessed | tf_op | source)
XLA Modules:
  0.0 533.6 jit_solution(17120316970074713340)
XLA Ops:
  25.8 38.2 %reduce-scatter.7.cloned.1.call-done = f32[64,1024]{1,0:T(8,128)} async-done(((f32[512,1024]{1,0:T(8,128)}), f32[64,1024]{1,0:T(8,128)}) %reduce-scatter.7.cloned.1.call-update) | async-done | bytes 262160
  68.4 13.2 %collective-permute-done = f32[64,1024]{0,1:T(8,128)S(1)} collective-permute-done((f32[64,1024]{0,1:T(8,128)S(1)}, f32[64,1024]{0,1:T(8,128)S(1)}, u32[]{:S(2)}, u32[]{:S(2)}) %collective-permute-start) | collective-permute-done | bytes 262176 | tf_op jit(solution)/shard_map/ppermute | solution.py:59
  81.9 5.5 %collective-permute-done.1 = f32[64,1024]{0,1:T(8,128)} collective-permute-done((f32[64,1024]{0,1:T(8,128)S(1)}, f32[64,1024]{0,1:T(8,128)}, u32[]{:S(2)}, u32[]{:S(2)}) %collective-permute-start.1) | collective-permute-done | bytes 262176 | tf_op jit(solution)/shard_map/ppermute | solution.py:64
  90.3 8.3 %collective-permute-done.2 = f32[64,1024]{0,1:T(8,128)} collective-permute-done((f32[64,1024]{0,1:T(8,128)S(1)}, f32[64,1024]{0,1:T(8,128)}, u32[]{:S(2)}, u32[]{:S(2)}) %collective-permute-start.2) | collective-permute-done | bytes 262176 | tf_op jit(solution)/shard_map/ppermute | solution.py:59
  105.2 8.1 %collective-permute-done.4 = f32[64,1024]{0,1:T(8,128)} collective-permute-done((f32[64,1024]{0,1:T(8,128)}, f32[64,1024]{0,1:T(8,128)}, u32[]{:S(2)}, u32[]{:S(2)}) %collective-permute-start.4) | collective-permute-done | bytes 262176 | tf_op jit(solution)/shard_map/ppermute | solution.py:59
  113.5 25.3 %all-reduce.5.cloned.1.call-done = f32[512,1024]{0,1:T(8,128)} async-done(((f32[512,1024]{0,1:T(8,128)}), f32[512,1024]{0,1:T(8,128)}) %all-reduce.5.cloned.1.call-update) | async-done | bytes 2097168 | tf_op jit(solution)/shard_map/psum | solution.py:9
  141.7 19.5 %scatter_custom_fusion = f32[512,1024]{1,0:T(8,128)S(1)} fusion(f32[512,1024]{1,0:T(8,128)S(1)} %copy.93, s32[512]{0:T(512)S(1)} %bitcast.75, f32[]{:T(128)} %constant.216.clone.4, pred[512]{0:T(512)(128)(4,1)S(1)} %compare_and_fusion.2, f32[512,1024]{1,0:T(8,128)} %copy.48, s32[1024]{0:T(1024)S(1)} %pad_clamp_fusion.2), kind=kCustom, calls=%fused_computation.17 | custom fusion | flops 524288 | bytes 4198916 | tf_op jit(solution)/shard_map/scatter | solution.py:79
  171.5 4.1 dynamic_update_slice.50
  182.4 4.1 dynamic_update_slice.53
  194.3 7.5 %fusion.2 = (f32[512,1024]{0,1:T(8,128)S(1)}, f32[1024,512]{1,0:T(8,128)}) fusion(f32[512,1024]{0,1:T(8,128)} %copy.49, f32[512,1024]{0,1:T(8,128)} %dynamic_update_slice.55, pred[1024]{0:T(1024)(128)(4,1)S(1)} %fusion.41, pred[]{:T(512)S(6)} %eq.82, f32[2,512,512]{2,1,0:T(8,128)} %param.20), kind=kOutput, calls=%fused_computation.12 | convolution fusion | flops 3222274048 | bytes 11535361 | tf_op jit(solution)/shard_map/dot_general | solution.py:29
  205.7 50.9 %all-reduce.7.cloned.1.call-done = f32[512,512]{0,1:T(8,128)} async-done(((f32[512,512]{0,1:T(8,128)}), f32[512,512]{0,1:T(8,128)}) %all-reduce.7.cloned.1.call-update) | async-done | bytes 1048592 | tf_op jit(solution)/shard_map/psum | solution.py:9
  256.6 6.9 %fusion.8 = f32[512,1024]{0,1:T(8,128)} fusion(f32[512,1024]{0,1:T(8,128)S(1)} %get-tuple-element.86, f32[1024,512]{1,0:T(8,128)} %get-tuple-element.87, f32[512,512]{0,1:T(8,128)} %all-reduce.7.cloned.1.call-done, pred[1024]{0:T(1024)(128)(4,1)S(1)} %fusion.41, pred[512]{0:T(512)(128)(4,1)S(1)} %get-tuple-element.90), kind=kOutput, calls=%fused_computation.20 | convolution fusion | flops 3222536192 | bytes 7341568 | tf_op jit(solution)/shard_map/dot_general | solution.py:29
  280.8 40.0 %reduce-scatter.9.cloned.1.call-done = f32[64,1024]{1,0:T(8,128)} async-done(((f32[512,1024]{1,0:T(8,128)}), f32[64,1024]{1,0:T(8,128)}) %reduce-scatter.9.cloned.1.call-update) | async-done | bytes 262160
  326.4 8.3 %collective-permute-done.7 = f32[64,1024]{0,1:T(8,128)S(1)} collective-permute-done((f32[64,1024]{0,1:T(8,128)S(1)}, f32[64,1024]{0,1:T(8,128)S(1)}, u32[]{:S(2)}, u32[]{:S(2)}) %collective-permute-start.7) | collective-permute-done | bytes 262176 | tf_op jit(solution)/shard_map/ppermute | solution.py:59
  335.2 10.4 %collective-permute-done.8 = f32[64,1024]{0,1:T(8,128)S(1)} collective-permute-done((f32[64,1024]{0,1:T(8,128)S(1)}, f32[64,1024]{0,1:T(8,128)S(1)}, u32[]{:S(2)}, u32[]{:S(2)}) %collective-permute-start.8) | collective-permute-done | bytes 262176 | tf_op jit(solution)/shard_map/ppermute | solution.py:64
  348.4 5.8 %collective-permute-done.9 = f32[64,1024]{0,1:T(8,128)S(1)} collective-permute-done((f32[64,1024]{0,1:T(8,128)S(1)}, f32[64,1024]{0,1:T(8,128)S(1)}, u32[]{:S(2)}, u32[]{:S(2)}) %collective-permute-start.9) | collective-permute-done | bytes 262176 | tf_op jit(solution)/shard_map/ppermute | solution.py:59
  354.3 6.5 %collective-permute-done.10 = f32[64,1024]{0,1:T(8,128)} collective-permute-done((f32[64,1024]{0,1:T(8,128)S(1)}, f32[64,1024]{0,1:T(8,128)}, u32[]{:S(2)}, u32[]{:S(2)}) %collective-permute-start.10) | collective-permute-done | bytes 262176 | tf_op jit(solution)/shard_map/ppermute | solution.py:64
  363.7 7.3 %collective-permute-done.11 = f32[64,1024]{0,1:T(8,128)} collective-permute-done((f32[64,1024]{0,1:T(8,128)S(1)}, f32[64,1024]{0,1:T(8,128)}, u32[]{:S(2)}, u32[]{:S(2)}) %collective-permute-start.11) | collective-permute-done | bytes 262176 | tf_op jit(solution)/shard_map/ppermute | solution.py:59
  371.0 25.0 %all-reduce.9.cloned.1.call-done = f32[512,1024]{0,1:T(8,128)} async-done(((f32[512,1024]{0,1:T(8,128)}), f32[512,1024]{0,1:T(8,128)}) %all-reduce.9.cloned.1.call-update) | async-done | bytes 2097168 | tf_op jit(solution)/shard_map/psum | solution.py:9
  398.9 19.8 %scatter_custom_fusion.1 = f32[512,1024]{1,0:T(8,128)S(1)} fusion(f32[512,1024]{1,0:T(8,128)S(1)} %copy.52, s32[512]{0:T(512)S(1)} %bitcast.74, f32[]{:T(128)} %constant.216.clone.4, pred[512]{0:T(512)(128)(4,1)S(1)} %compare_and_fusion, f32[512,1024]{1,0:T(8,128)} %copy.54, s32[1024]{0:T(1024)S(1)} %pad_clamp_fusion), kind=kCustom, calls=%fused_computation.14 | custom fusion | flops 524288 | bytes 4198916 | tf_op jit(solution)/shard_map/scatter | solution.py:79
  439.6 4.1 dynamic_update_slice.61
  451.8 8.2 %fusion = (f32[512,1024]{0,1:T(8,128)S(1)}, f32[1024,512]{1,0:T(8,128)}) fusion(f32[512,1024]{0,1:T(8,128)} %copy.56, f32[512,1024]{0,1:T(8,128)} %dynamic_update_slice.63, pred[1024]{0:T(1024)(128)(4,1)S(1)} %fusion.42, pred[]{:T(512)S(6)} %eq.81, f32[2,512,512]{2,1,0:T(8,128)} %param.20), kind=kOutput, calls=%fused_computation.8 | convolution fusion | flops 3222274048 | bytes 11535361 | tf_op jit(solution)/shard_map/dot_general | solution.py:29
  462.9 51.1 %all-reduce.11.cloned.1.call-done = f32[512,512]{0,1:T(8,128)} async-done(((f32[512,512]{0,1:T(8,128)}), f32[512,512]{0,1:T(8,128)}) %all-reduce.11.cloned.1.call-update) | async-done | bytes 1048592 | tf_op jit(solution)/shard_map/psum | solution.py:9
  514.1 6.9 %fusion.9 = f32[512,1024]{0,1:T(8,128)} fusion(f32[512,1024]{0,1:T(8,128)S(1)} %get-tuple-element.88, f32[1024,512]{1,0:T(8,128)} %get-tuple-element.89, f32[512,512]{0,1:T(8,128)} %all-reduce.11.cloned.1.call-done, pred[1024]{0:T(1024)(128)(4,1)S(1)} %fusion.42, pred[512]{0:T(512)(128)(4,1)S(1)} %fusion.43), kind=kOutput, calls=%fused_computation.21 | convolution fusion | flops 3222536192 | bytes 7341568 | tf_op jit(solution)/shard_map/dot_general | solution.py:29
  (125 shorter events, 134.1 us)
Async XLA Ops:
  6.5 57.4 %reduce-scatter.7.cloned.1.call-start = ((), (), s32[]{:S(2)}) async-start(), calls=%async_computation.6 | async-start | bytes 2359296
  19.9 118.9 %all-reduce.5.cloned.1.call-start = ((), (), s32[]{:S(2)}) async-start(), calls=%async_computation.2 | async-start | bytes 4194304 | tf_op jit(solution)/shard_map/psum | solution.py:9
  24.9 231.7 %all-reduce.7.cloned.1.call-start = ((), (), s32[]{:S(2)}) async-start(), calls=%async_computation.3 | async-start | bytes 2097152 | tf_op jit(solution)/shard_map/psum | solution.py:9
  65.1 16.4 %collective-permute-start = (f32[64,1024]{0,1:T(8,128)S(1)}, f32[64,1024]{0,1:T(8,128)S(1)}, u32[]{:S(2)}, u32[]{:S(2)}) collective-permute-start(f32[64,1024]{0,1:T(8,128)S(1)} %copy.65), channel_id=1, source_target_pairs={{0,4},{4,8},{8,12},{12,16},{16,20},{20,24},{24,28},{28,0},{1,5},{5... | collective-permute-start | bytes 786440 | tf_op jit(solution)/shard_map/ppermute | solution.py:59
  65.7 21.7 %collective-permute-start.1 = (f32[64,1024]{0,1:T(8,128)S(1)}, f32[64,1024]{0,1:T(8,128)}, u32[]{:S(2)}, u32[]{:S(2)}) collective-permute-start(f32[64,1024]{0,1:T(8,128)S(1)} %copy.65), channel_id=1, source_target_pairs={{0,28},{4,0},{8,4},{12,8},{16,12},{20,16},{24,20},{28,24},{1,29},{... | collective-permute-start | bytes 786440 | tf_op jit(solution)/shard_map/ppermute | solution.py:64
  81.5 17.1 %collective-permute-start.2 = (f32[64,1024]{0,1:T(8,128)S(1)}, f32[64,1024]{0,1:T(8,128)}, u32[]{:S(2)}, u32[]{:S(2)}) collective-permute-start(f32[64,1024]{0,1:T(8,128)S(1)} %collective-permute-done), channel_id=1, source_target_pairs={{0,4},{4,8},{8,12},{12,16},{16,20},{20,24},{24,28},{28,0},{1,5},{5... | collective-permute-start | bytes 786440 | tf_op jit(solution)/shard_map/ppermute | solution.py:59
  87.4 15.0 %collective-permute-start.3 = (f32[64,1024]{0,1:T(8,128)}, f32[64,1024]{0,1:T(8,128)}, u32[]{:S(2)}, u32[]{:S(2)}) collective-permute-start(f32[64,1024]{0,1:T(8,128)} %collective-permute-done.1), channel_id=1, source_target_pairs={{0,28},{4,0},{8,4},{12,8},{16,12},{20,16},{24,20},{28,24},{1,29},{... | collective-permute-start | bytes 786440 | tf_op jit(solution)/shard_map/ppermute | solution.py:64
  98.6 14.7 %collective-permute-start.4 = (f32[64,1024]{0,1:T(8,128)}, f32[64,1024]{0,1:T(8,128)}, u32[]{:S(2)}, u32[]{:S(2)}) collective-permute-start(f32[64,1024]{0,1:T(8,128)} %collective-permute-done.2), channel_id=1, source_target_pairs={{0,4},{4,8},{8,12},{12,16},{16,20},{20,24},{24,28},{28,0},{1,5},{5... | collective-permute-start | bytes 786440 | tf_op jit(solution)/shard_map/ppermute | solution.py:59
  102.4 84.1 %collective-permute-start.5 = (f32[64,1024]{0,1:T(8,128)}, f32[64,1024]{0,1:T(8,128)}, u32[]{:S(2)}, u32[]{:S(2)}) collective-permute-start(f32[64,1024]{0,1:T(8,128)} %collective-permute-done.3), channel_id=1, source_target_pairs={{0,28},{4,0},{8,4},{12,8},{16,12},{20,16},{24,20},{28,24},{1,29},{... | collective-permute-start | bytes 786440 | tf_op jit(solution)/shard_map/ppermute | solution.py:64
  113.3 77.3 %collective-permute-start.6 = (f32[64,1024]{0,1:T(8,128)}, f32[64,1024]{0,1:T(8,128)}, u32[]{:S(2)}, u32[]{:S(2)}) collective-permute-start(f32[64,1024]{0,1:T(8,128)} %collective-permute-done.4), channel_id=1, source_target_pairs={{0,4},{4,8},{8,12},{12,16},{16,20},{20,24},{24,28},{28,0},{1,5},{5... | collective-permute-start | bytes 786440 | tf_op jit(solution)/shard_map/ppermute | solution.py:59
  204.8 116.0 %reduce-scatter.9.cloned.1.call-start = ((), (), s32[]{:S(2)}) async-start(), calls=%async_computation.7 | async-start | bytes 2359296
  280.0 116.0 %all-reduce.9.cloned.1.call-start = ((), (), s32[]{:S(2)}) async-start(), calls=%async_computation.4 | async-start | bytes 4194304 | tf_op jit(solution)/shard_map/psum | solution.py:9
  321.9 12.8 %collective-permute-start.7 = (f32[64,1024]{0,1:T(8,128)S(1)}, f32[64,1024]{0,1:T(8,128)S(1)}, u32[]{:S(2)}, u32[]{:S(2)}) collective-permute-start(f32[64,1024]{0,1:T(8,128)S(1)} %copy.67), channel_id=1, source_target_pairs={{0,4},{4,8},{8,12},{12,16},{16,20},{20,24},{24,28},{28,0},{1,5},{5... | collective-permute-start | bytes 786440 | tf_op jit(solution)/shard_map/ppermute | solution.py:59
  323.6 190.5 %all-reduce.11.cloned.1.call-start = ((), (), s32[]{:S(2)}) async-start(), calls=%async_computation.5 | async-start | bytes 2097152 | tf_op jit(solution)/shard_map/psum | solution.py:9
  323.8 21.9 %collective-permute-start.8 = (f32[64,1024]{0,1:T(8,128)S(1)}, f32[64,1024]{0,1:T(8,128)S(1)}, u32[]{:S(2)}, u32[]{:S(2)}) collective-permute-start(f32[64,1024]{0,1:T(8,128)S(1)} %copy.67), channel_id=1, source_target_pairs={{0,28},{4,0},{8,4},{12,8},{16,12},{20,16},{24,20},{28,24},{1,29},{... | collective-permute-start | bytes 786440 | tf_op jit(solution)/shard_map/ppermute | solution.py:64
  334.8 19.5 %collective-permute-start.9 = (f32[64,1024]{0,1:T(8,128)S(1)}, f32[64,1024]{0,1:T(8,128)S(1)}, u32[]{:S(2)}, u32[]{:S(2)}) collective-permute-start(f32[64,1024]{0,1:T(8,128)S(1)} %collective-permute-done.7), channel_id=1, source_target_pairs={{0,4},{4,8},{8,12},{12,16},{16,20},{20,24},{24,28},{28,0},{1,5},{5... | collective-permute-start | bytes 786440 | tf_op jit(solution)/shard_map/ppermute | solution.py:59
  345.6 8.6 %copy-start.4 = (f32[64,1024]{0,1:T(8,128)}, f32[64,1024]{0,1:T(8,128)S(1)}, u32[]{:S(2)}) copy-start(f32[64,1024]{0,1:T(8,128)S(1)} %collective-permute-done.8) | copy-start | bytes 786436
  345.6 15.2 %collective-permute-start.10 = (f32[64,1024]{0,1:T(8,128)S(1)}, f32[64,1024]{0,1:T(8,128)}, u32[]{:S(2)}, u32[]{:S(2)}) collective-permute-start(f32[64,1024]{0,1:T(8,128)S(1)} %collective-permute-done.8), channel_id=1, source_target_pairs={{0,28},{4,0},{8,4},{12,8},{16,12},{20,16},{24,20},{28,24},{1,29},{... | collective-permute-start | bytes 786440 | tf_op jit(solution)/shard_map/ppermute | solution.py:64
  354.2 16.7 %collective-permute-start.11 = (f32[64,1024]{0,1:T(8,128)S(1)}, f32[64,1024]{0,1:T(8,128)}, u32[]{:S(2)}, u32[]{:S(2)}) collective-permute-start(f32[64,1024]{0,1:T(8,128)S(1)} %collective-permute-done.9), channel_id=1, source_target_pairs={{0,4},{4,8},{8,12},{12,16},{16,20},{20,24},{24,28},{28,0},{1,5},{5... | collective-permute-start | bytes 786440 | tf_op jit(solution)/shard_map/ppermute | solution.py:59
  360.8 82.9 %collective-permute-start.12 = (f32[64,1024]{0,1:T(8,128)}, f32[64,1024]{0,1:T(8,128)}, u32[]{:S(2)}, u32[]{:S(2)}) collective-permute-start(f32[64,1024]{0,1:T(8,128)} %collective-permute-done.10), channel_id=1, source_target_pairs={{0,28},{4,0},{8,4},{12,8},{16,12},{20,16},{24,20},{28,24},{1,29},{... | collective-permute-start | bytes 786440 | tf_op jit(solution)/shard_map/ppermute | solution.py:64
  371.0 76.8 %collective-permute-start.13 = (f32[64,1024]{0,1:T(8,128)}, f32[64,1024]{0,1:T(8,128)}, u32[]{:S(2)}, u32[]{:S(2)}) collective-permute-start(f32[64,1024]{0,1:T(8,128)} %collective-permute-done.11), channel_id=1, source_target_pairs={{0,4},{4,8},{8,12},{12,16},{16,20},{20,24},{24,28},{28,0},{1,5},{5... | collective-permute-start | bytes 786440 | tf_op jit(solution)/shard_map/ppermute | solution.py:59
  420.6 8.5 %copy-start.5 = (f32[64,1024]{0,1:T(8,128)S(1)}, f32[64,1024]{0,1:T(8,128)}, u32[]{:S(2)}) copy-start(f32[64,1024]{0,1:T(8,128)} %copy-done.4) | copy-start | bytes 786436
  422.2 10.9 %copy-start.7 = (f32[64,1024]{0,1:T(8,128)S(1)}, f32[64,1024]{0,1:T(8,128)}, u32[]{:S(2)}) copy-start(f32[64,1024]{0,1:T(8,128)} %copy-done.6) | copy-start | bytes 786436
  451.8 8.2 %copy-start.3 = (f32[2,512,512]{2,1,0:T(8,128)S(1)}, f32[2,512,512]{2,1,0:T(8,128)}, u32[]{:S(2)}) copy-start(f32[2,512,512]{2,1,0:T(8,128)} %param.21) | copy-start | bytes 6291460
  (5 other events, 29.5 us)
Sparse Core Ops, SparseCore 0:
  20.0 43.8 reduce-scatter.6
  67.5 71.2 all-reduce.4
  204.9 51.6 all-reduce.6
  280.2 40.5 reduce-scatter.8
  324.2 71.7 all-reduce.8
  463.0 51.0 all-reduce.10
